TPU v7x, 256 devices: a whole 4x4x8 slice. The times are simulated.
256 devices in a mesh: dp: 32 (over z_hi, y, core), rows: 8 (over z_lo, x).
Axes of the slice: x: 4, y: 4, z: 8 (z_hi: 4, z_lo: 2; z = z_hi * 2 + z_lo), core: 2. Of those that a mesh axis runs over, the one named last changes fastest.
Arguments:
- latent: bfloat16 [32, 320, 16, 128], P('dp', None, 'rows'), may hold values from -14 to 14
- hint_field: bfloat16 [32, 320, 16, 128], P('dp', None, 'rows'), may hold values from -6 to 6
- from_below: bfloat16 [32, 320, 16, 128], P('dp', None, 'rows'), may hold values from -6 to 6
- cotangent: bfloat16 [32, 320, 16, 128], P('dp', None, 'rows'), may hold values from -6 to 6
- timesteps: int32 [32], P('dp'), may hold values from 0 to 999
- time_weight: bfloat16 [320, 1280], replicated, may hold values from -0.3125 to 0.3125
- enc_proj: bfloat16 [1280, 320], replicated, may hold values from -0.4375 to 0.4375
- ctl_proj: bfloat16 [1280, 320], replicated, may hold values from -0.15625 to 0.15625
- dec_proj: bfloat16 [1280, 320], replicated, may hold values from -0.15625 to 0.15625
- enc_conv_one: bfloat16 [320, 3, 3, 320], replicated, may hold values from -0.109375 to 0.109375
- enc_conv_two: bfloat16 [320, 3, 3, 320], replicated, may hold values from -0.109375 to 0.109375
- ctl_conv_one: bfloat16 [320, 3, 3, 320], P('dp'), may hold values from -0.109375 to 0.109375
- ctl_conv_two: bfloat16 [320, 3, 3, 320], P('dp'), may hold values from -0.109375 to 0.109375
- dec_conv_one: bfloat16 [320, 3, 3, 640], P('dp'), may hold values from -0.078125 to 0.078125
- dec_conv_two: bfloat16 [320, 3, 3, 320], P('dp'), may hold values from -0.109375 to 0.109375
- dec_shortcut: bfloat16 [320, 640], P('dp'), may hold values from -0.25 to 0.25
- zero_conv: bfloat16 [320, 320], P('dp'), may hold values from -0.3125 to 0.3125
Outputs:
- ctl_conv_one_grad: float32 [320, 3, 3, 320], P('dp')
- ctl_conv_two_grad: float32 [320, 3, 3, 320], P('dp')
- zero_conv_grad: float32 [320, 320], P('dp')
All inputs are finite; a program needn't handle non-finite values.
Results may differ from a plain program's by a relative error of at most 0.009.
Values may be sent and summed in bfloat16 or wider, within the bound.
A program may use at most 128 MiB of HBM per device.

v0:
```python
import math
import jax
import jax.numpy as jnp
from jax import lax
from jax.sharding import PartitionSpec as P

C = 320
GROUPS = 32
EPSILON = 1e-05
LAYOUT = ("NCHW", "OHWI", "NCHW")


def extended(x, sides, width):
    for axis, dim in sides:
        peers, length = (lax.axis_size(axis), x.shape[dim])
        up = [(i, (i + 1) % peers) for i in range(peers - 1)]
        down = [(j, i) for i, j in up]
        last = lax.slice_in_dim(x, length - width, length, axis=dim)
        first = lax.slice_in_dim(x, 0, width, axis=dim)
        before = lax.ppermute(last, axis, up)
        after = lax.ppermute(first, axis, down)
        x = jnp.concatenate([before, x, after], axis=dim)
    return x


def shifted(value, axis, steps):
    count = lax.axis_size(axis)
    first, last = (max(0, -steps), min(count, count - steps))
    return lax.ppermute(value, axis, [(source, source + steps) for source in range(first, last)])


def conv_rows(padded, weight):
    return lax.conv_general_dilated(
        padded,
        weight,
        (1, 1),
        ((0, 0), (1, 1)),
        dimension_numbers=LAYOUT,
        preferred_element_type=jnp.float32,
    )


def with_halo(source):
    return extended(source, (("rows", 2),), 1)


def mix_channels(matrix, source):
    return jnp.einsum("oi,bihw->bohw", matrix, source, preferred_element_type=jnp.float32)


def mix_back(matrix, upstream):
    return jnp.einsum("oi,bohw->bihw", matrix, upstream, preferred_element_type=jnp.float32)


def flip_kernel(weight):
    return jnp.transpose(weight[:, ::-1, ::-1, :], (3, 1, 2, 0))


def group_norm(source):
    full_shape = source.shape
    grouped = source.reshape(
        full_shape[0], GROUPS, full_shape[1] // GROUPS, full_shape[2], full_shape[3]
    )
    group_count = full_shape[1] // GROUPS * full_shape[2] * full_shape[3] * lax.axis_size("rows")
    group_total, group_square = lax.psum(
        (jnp.sum(grouped, axis=(2, 3, 4)), jnp.sum(grouped * grouped, axis=(2, 3, 4))), "rows"
    )
    average = group_total / group_count
    inv_spread = lax.rsqrt(group_square / group_count - average * average + EPSILON)
    normed = (grouped - average[:, :, None, None, None]) * inv_spread[:, :, None, None, None]
    return (normed.reshape(full_shape), inv_spread)


def norm_back(upstream, normed, inv_spread):
    full_shape = upstream.shape
    groups_here = inv_spread.shape[1]
    grouped = upstream.reshape(
        full_shape[0], groups_here, full_shape[1] // groups_here, full_shape[2], full_shape[3]
    )
    normed_grouped = normed.reshape(grouped.shape)
    group_count = (
        full_shape[1] // groups_here * full_shape[2] * full_shape[3] * lax.axis_size("rows")
    )
    group_total, group_cross = lax.psum(
        (jnp.sum(grouped, axis=(2, 3, 4)), jnp.sum(grouped * normed_grouped, axis=(2, 3, 4))),
        "rows",
    )
    first_mean = (group_total / group_count)[:, :, None, None, None]
    cross_mean = (group_cross / group_count)[:, :, None, None, None]
    result = inv_spread[:, :, None, None, None] * (
        grouped - first_mean - normed_grouped * cross_mean
    )
    return result.reshape(full_shape)


def silu_slope(values):
    sigma = jax.nn.sigmoid(values)
    return sigma * (1.0 + values * (1.0 - sigma))


def input_grad(upstream, weight):
    flipped = flip_kernel(weight)
    padded = jnp.pad(upstream, ((0, 0), (0, 0), (2, 2), (0, 0)))
    spilled = conv_rows(padded, flipped)
    from_next = shifted(spilled[:, :, :1], "rows", -1)
    from_prev = shifted(spilled[:, :, -1:], "rows", 1)
    result = spilled[:, :, 1:-1]
    result = result.at[:, :, :1].add(from_prev)
    result = result.at[:, :, -1:].add(from_next)
    return result


def kernel_grad(upstream, padded):
    wide = jnp.pad(padded, ((0, 0), (0, 0), (0, 0), (1, 1)))
    row_count = upstream.shape[2]
    col_count = upstream.shape[3]
    return jnp.stack(
        [
            jnp.stack(
                [
                    jnp.einsum(
                        "bohw,bihw->oi",
                        upstream,
                        wide[:, :, row_tap : row_tap + row_count, col_tap : col_tap + col_count],
                        preferred_element_type=jnp.float32,
                    )
                    for col_tap in range(3)
                ],
                1,
            )
            for row_tap in range(3)
        ],
        1,
    )


def block_front(source, conv_one, time_term):
    normed_in, spread_in = group_norm(source.astype(jnp.float32))
    first_halo = with_halo(jax.nn.silu(normed_in).astype(jnp.bfloat16))
    inner_sum = conv_rows(first_halo, conv_one) + time_term[:, :, None, None]
    normed, spread = group_norm(inner_sum)
    second_act = jax.nn.silu(normed).astype(jnp.bfloat16)
    return (normed_in, spread_in, first_halo, normed, spread, second_act)


def per_device(
    latent,
    hint_field,
    from_below,
    cotangent,
    timesteps,
    time_weight,
    enc_proj,
    ctl_proj,
    dec_proj,
    enc_conv_one,
    enc_conv_two,
    ctl_conv_one,
    ctl_conv_two,
    dec_conv_one,
    dec_conv_two,
    dec_shortcut,
    zero_conv,
):
    ctl_one, ctl_two, dec_one, dec_two, dec_short, zero_full = (
        lax.all_gather(ctl_conv_one, "dp", axis=0, tiled=True),
        lax.all_gather(ctl_conv_two, "dp", axis=0, tiled=True),
        lax.all_gather(dec_conv_one, "dp", axis=0, tiled=True),
        lax.all_gather(dec_conv_two, "dp", axis=0, tiled=True),
        lax.all_gather(dec_shortcut, "dp", axis=0, tiled=True),
        lax.all_gather(zero_conv, "dp", axis=0, tiled=True),
    )
    half_width = C // 2
    frequency = jnp.exp(-math.log(10000.0) * jnp.arange(half_width, dtype=jnp.float32) / half_width)
    angles = timesteps.astype(jnp.float32)[:, None] * frequency[None, :]
    sinusoid = jnp.concatenate([jnp.cos(angles), jnp.sin(angles)], axis=1).astype(jnp.bfloat16)
    time_embed = jnp.dot(sinusoid, time_weight, preferred_element_type=jnp.float32)
    time_act = jax.nn.silu(time_embed).astype(jnp.bfloat16)
    enc_term = jnp.dot(time_act, enc_proj, preferred_element_type=jnp.float32)
    ctl_term = jnp.dot(time_act, ctl_proj, preferred_element_type=jnp.float32)
    dec_term = jnp.dot(time_act, dec_proj, preferred_element_type=jnp.float32)
    enc_parts = block_front(latent, enc_conv_one, enc_term)
    enc_out = (
        latent.astype(jnp.float32) + conv_rows(with_halo(enc_parts[5]), enc_conv_two)
    ).astype(jnp.bfloat16)
    ctl_in = (latent.astype(jnp.float32) + hint_field.astype(jnp.float32)).astype(jnp.bfloat16)
    ctl_parts = block_front(ctl_in, ctl_one, ctl_term)
    ctl_halo = with_halo(ctl_parts[5])
    ctl_out = (ctl_in.astype(jnp.float32) + conv_rows(ctl_halo, ctl_two)).astype(jnp.bfloat16)
    skip_sum = (enc_out.astype(jnp.float32) + mix_channels(zero_full, ctl_out)).astype(jnp.bfloat16)
    joined = jnp.concatenate([from_below, skip_sum], axis=1)
    dec_parts = block_front(joined, dec_one, dec_term)
    loss_scale = float(
        cotangent.shape[0]
        * lax.axis_size("dp")
        * cotangent.shape[2]
        * lax.axis_size("rows")
        * cotangent.shape[3]
    ) ** (-0.5)
    out_grad = (cotangent.astype(jnp.float32) * loss_scale).astype(jnp.bfloat16)
    dec_second_grad = input_grad(out_grad, dec_two)
    dec_inner_grad = norm_back(
        dec_second_grad * silu_slope(dec_parts[3]), dec_parts[3], dec_parts[4]
    ).astype(jnp.bfloat16)
    skip_first_grad = input_grad(dec_inner_grad, dec_one[:, :, :, C:])
    skip_normed = dec_parts[0][:, C:]
    skip_spread = dec_parts[1][:, GROUPS // 2 :]
    skip_grad = norm_back(
        skip_first_grad * silu_slope(skip_normed), skip_normed, skip_spread
    ) + mix_back(dec_short[:, C:], out_grad)
    skip_grad = skip_grad.astype(jnp.bfloat16)
    zero_local = jnp.einsum("bohw,bihw->oi", skip_grad, ctl_out, preferred_element_type=jnp.float32)
    ctl_out_grad = mix_back(zero_full, skip_grad).astype(jnp.bfloat16)
    two_local = kernel_grad(ctl_out_grad, ctl_halo)
    ctl_second_grad = input_grad(ctl_out_grad, ctl_two)
    ctl_inner_grad = norm_back(
        ctl_second_grad * silu_slope(ctl_parts[3]), ctl_parts[3], ctl_parts[4]
    ).astype(jnp.bfloat16)
    one_local = kernel_grad(ctl_inner_grad, ctl_parts[2])
    owned = (
        lax.psum_scatter(one_local, "dp", scatter_dimension=0, tiled=True),
        lax.psum_scatter(two_local, "dp", scatter_dimension=0, tiled=True),
        lax.psum_scatter(zero_local, "dp", scatter_dimension=0, tiled=True),
    )
    one_grad, two_grad, zero_grad = lax.psum((owned[0], owned[1], owned[2]), "rows")
    return (one_grad, two_grad, zero_grad)


def solution(mesh):
    in_specs = (
        P("dp", None, "rows", None),
        P("dp", None, "rows", None),
        P("dp", None, "rows", None),
        P("dp", None, "rows", None),
        P("dp"),
        P(),
        P(),
        P(),
        P(),
        P(),
        P(),
        P("dp", None, None, None),
        P("dp", None, None, None),
        P("dp", None, None, None),
        P("dp", None, None, None),
        P("dp", None),
        P("dp", None),
    )
    out_specs = (P("dp", None, None, None), P("dp", None, None, None), P("dp", None))
    return jax.shard_map(
        per_device, mesh=mesh, in_specs=in_specs, out_specs=out_specs, check_vma=False
    )
```

profile of v0, /device:TPU:8, one launch (start us, length us, event | category | flops | bytes accessed | tf_op | source)
XLA Modules:
  0.0 869.3 jit_solution(10912018785608878271)
XLA Ops:
  9.5 1.3 convert_reduce_fusion.1
  11.7 20.1 %all-reduce.12 = (f32[1,32]{1,0:T(1,128)S(1)}, f32[1,32]{1,0:T(1,128)S(1)}, f32[1,32]{1,0:T(1,128)S(1)}, f32[1,32]{1,0:T(1,128)S(1)}) all-reduce(f32[1,32]{1,0:T(1,128)S(1)} %bitcast.481, f32[1,32]{1,0:T(1,128)S(1)} %bitcast.476, f32[1,32]{1,0:T(1,128)S(1)} %bitcast.479, ...), channel_id=1, replica_groups=mesh['dp'=32,'rows'=8] {'rows'}, use_global_device_ids=true, to_apply=%region_5.6 | all-reduce | flops 128 | bytes 1024 | tf_op jit(solution)/shard_map/psum | solution.py:65
  33.0 1.3 collective-permute-start
  34.3 1.3 collective-permute-start.1
  37.8 5.3 collective-permute-start.2
  43.1 1.3 collective-permute-start.3
  44.4 43.7 %all-gather = bf16[32,10,320]{2,1,0:T(8,128)(2,1)S(1)} all-gather(bf16[1,10,320]{2,1,0:T(8,128)(2,1)S(1)} %bitcast.473), channel_id=1, replica_groups=mesh['dp'=32,'rows'=8] {'dp'}, dimensions={0}, use_global_device_ids=true | all-gather | bytes 211200 | tf_op jit(solution)/shard_map/all_gather | solution.py:171
  90.6 1.4 convolution_reduce_fusion
  92.1 2.1 convolution_reduce_fusion.3
  94.1 1.5 convolution_reduce_fusion.2
  96.3 1.8 fusion.188
  99.2 49.5 %all-gather.1 = bf16[32,10,640]{2,1,0:T(8,128)(2,1)S(1)} all-gather(bf16[1,10,640]{2,1,0:T(8,128)(2,1)S(1)} %bitcast.472), channel_id=1, replica_groups=mesh['dp'=32,'rows'=8] {'dp'}, dimensions={0}, use_global_device_ids=true | all-gather | bytes 422400 | tf_op jit(solution)/shard_map/all_gather | solution.py:170
  149.6 1.5 convolution_reduce_fusion.1
  151.8 1.7 pad_maximum_fusion.2
  155.7 1.7 maximum_bitcast_fusion.8
  159.0 3.1 fusion.27
  162.1 2.0 select_reduce_fusion.3
  165.0 21.3 %all-reduce.11 = (f32[1,32]{1,0:T(1,128)S(1)}, f32[1,32]{1,0:T(1,128)S(1)}, f32[1,32]{1,0:T(1,128)S(1)}, f32[1,32]{1,0:T(1,128)S(1)}) all-reduce(f32[1,32]{1,0:T(1,128)S(1)} %bitcast.480, f32[1,32]{1,0:T(1,128)S(1)} %bitcast.482, f32[1,32]{1,0:T(1,128)S(1)} %bitcast.478, ...), channel_id=1, replica_groups=mesh['dp'=32,'rows'=8] {'rows'}, use_global_device_ids=true, to_apply=%region_8.9 | all-reduce | flops 128 | bytes 1024 | tf_op jit(solution)/shard_map/psum | solution.py:65
  190.1 1.3 collective-permute-start.6
  192.3 1.3 collective-permute-start.7
  195.6 1.3 collective-permute-start.5
  197.6 6.0 collective-permute-start.4
  203.7 3.7 fusion.14
  208.4 4.0 collective-permute-start.10
  215.0 1.3 collective-permute-start.11
  217.7 3.1 fusion.20
  222.6 1.6 maximum_bitcast_fusion.7
  227.0 1.4 fusion.34
  229.0 22.0 %all-reduce.10 = (f32[1,32]{1,0:T(1,128)S(1)}, f32[1,32]{1,0:T(1,128)S(1)}) all-reduce(f32[1,32]{1,0:T(1,128)S(1)} %bitcast.484, f32[1,32]{1,0:T(1,128)S(1)} %bitcast.489), channel_id=1, replica_groups=mesh['dp'=32,'rows'=8] {'rows'}, use_global_device_ids=true, to_apply=%region_26.27 | all-reduce | flops 64 | bytes 512 | tf_op jit(solution)/shard_map/psum | solution.py:65
  253.3 1.3 collective-permute-start.8
  254.6 1.5 collective-permute-start.9
  256.1 1.8 fusion.131
  257.9 4.0 scatter-add.20
  261.9 1.2 slice_add_fusion.1
  263.2 2.8 scatter-add.21
  266.0 1.9 maximum_bitcast_fusion.6
  267.9 1.6 copy.299
  269.9 2.9 copy.236
  272.8 2.7 select_reduce_fusion.1
  275.9 21.8 %all-reduce.9 = (f32[1,32]{1,0:T(1,128)S(1)}, f32[1,32]{1,0:T(1,128)S(1)}) all-reduce(f32[1,32]{1,0:T(1,128)S(1)} %bitcast.486, f32[1,32]{1,0:T(1,128)S(1)} %bitcast.490), channel_id=1, replica_groups=mesh['dp'=32,'rows'=8] {'rows'}, use_global_device_ids=true, to_apply=%region_32.33 | all-reduce | flops 64 | bytes 512 | tf_op jit(solution)/shard_map/psum | solution.py:65
  300.5 18.9 %all-reduce.8 = (f32[1,32]{1,0:T(1,128)S(1)}, f32[1,32]{1,0:T(1,128)S(1)}) all-reduce(f32[1,32]{1,0:T(1,128)S(1)} %bitcast.491, f32[1,32]{1,0:T(1,128)S(1)} %bitcast.485), channel_id=1, replica_groups=mesh['dp'=32,'rows'=8] {'rows'}, use_global_device_ids=true, to_apply=%region_41.42 | all-reduce | flops 64 | bytes 512 | tf_op jit(solution)/shard_map/psum | solution.py:84
  320.6 3.5 fusion.17
  326.0 1.9 collective-permute-start.12
  332.3 1.3 collective-permute-start.13
  334.6 4.9 collective-permute-done.13
  340.9 20.5 %all-reduce.7 = (f32[1,16]{1,0:T(1,128)S(1)}, f32[1,16]{1,0:T(1,128)S(1)}) all-reduce(f32[1,16]{1,0:T(1,128)S(1)} %bitcast.492, f32[1,16]{1,0:T(1,128)S(1)} %bitcast.487), channel_id=1, replica_groups=mesh['dp'=32,'rows'=8] {'rows'}, use_global_device_ids=true, to_apply=%region_47.48 | all-reduce | flops 32 | bytes 256 | tf_op jit(solution)/shard_map/psum | solution.py:84
  361.7 1.7 fusion.35
  363.4 1.2 convolution_convert_fusion
  372.2 3.7 fusion.11
  376.3 1.7 collective-permute-start.14
  381.4 5.5 copy.283
  387.1 1.5 collective-permute-start.15
  389.9 2.8 scatter-add.26
  392.8 2.4 collective-permute-done.15
  395.5 2.8 scatter-add.29
  399.2 22.1 %all-reduce.6 = (f32[1,32]{1,0:T(1,128)S(1)}, f32[1,32]{1,0:T(1,128)S(1)}) all-reduce(f32[1,32]{1,0:T(1,128)S(1)} %bitcast.488, f32[1,32]{1,0:T(1,128)S(1)} %bitcast.483), channel_id=1, replica_groups=mesh['dp'=32,'rows'=8] {'rows'}, use_global_device_ids=true, to_apply=%region_53.54 | all-reduce | flops 64 | bytes 512 | tf_op jit(solution)/shard_map/psum | solution.py:84
  426.9 5.5 copy.282
  434.3 335.3 %all-reduce.17.cloned.1.call-done = (f32[320,3,3,320]{3,2,1,0:T(4,128)}, f32[320,3,3,320]{3,2,1,0:T(4,128)}, f32[320,320]{1,0:T(8,128)}) async-done(((f32[320,3,3,320]{3,2,1,0:T(4,128)}, f32[320,3,3,320]{3,2,1,0:T(4,128)}, f32[320,320]{1,0:T(8,128)}), (f32[320,3,3,320]{3,2,1,0:T(4,128)}, f32[320,3,3,320]{3,2,1,0:T(4,128)}, f32[320,320]{1,0:T(8,128)})) %all-reduce.17.cloned.1.call-update) | async-done | bytes 7782416
  769.7 1.6 constant_dynamic-slice_fusion.1
  771.3 1.6 constant_dynamic-slice_fusion.2
  773.7 37.2 %psum.167 = f32[10,320]{1,0:T(8,128)} all-reduce(f32[10,320]{1,0:T(8,128)S(1)} %constant_dynamic-slice_fusion), channel_id=1, replica_groups=mesh['dp'=32,'rows'=8] {'rows'}, use_global_device_ids=true, to_apply=%region_59.60 | all-reduce | flops 3200 | bytes 25600 | tf_op jit(solution)/shard_map/psum | solution.py:225
  810.9 48.1 %all-reduce.19.cloned.1.call-done = (f32[10,3,3,320]{3,2,1,0:T(4,128)}, f32[10,3,3,320]{3,2,1,0:T(4,128)}) async-done(((f32[10,3,3,320]{3,2,1,0:T(4,128)}, f32[10,3,3,320]{3,2,1,0:T(4,128)}), (f32[10,3,3,320]{3,2,1,0:T(4,128)}, f32[10,3,3,320]{3,2,1,0:T(4,128)})) %all-reduce.19.cloned.1.call-update) | async-done | bytes 230416 | tf_op jit(solution)/shard_map/psum | solution.py:225
  859.0 1.6 copy.342
  860.6 1.6 copy.343
  (354 shorter events, 70.5 us)
Async XLA Ops:
  7.2 154.9 %copy-start = (bf16[320,3,3,320]{3,0,2,1:T(8,128)(2,1)S(1)}, bf16[320,3,3,320]{3,0,2,1:T(8,128)(2,1)}, u32[]{:S(2)}) copy-start(bf16[320,3,3,320]{3,0,2,1:T(8,128)(2,1)} %param.38) | copy-start | bytes 5529604
  7.2 37.2 %copy-start.34 = (bf16[10,320]{1,0:T(8,128)(2,1)S(1)}, bf16[10,320]{1,0:T(8,128)(2,1)}, u32[]{:S(2)}) copy-start(bf16[10,320]{1,0:T(8,128)(2,1)} %param.45) | copy-start | bytes 19204
  7.2 151.8 %all-gather.7.cloned.1.call-start = ((), (), s32[]{:S(2)}) async-start(), calls=%async_computation | async-start | bytes 3041280 | tf_op jit(solution)/shard_map/all_gather | solution.py:166
  7.9 195.7 %all-gather.13.cloned.1.call-start = ((), (), s32[]{:S(2)}) async-start(), calls=%async_computation.3 | async-start | bytes 3041280 | tf_op jit(solution)/shard_map/all_gather | solution.py:169
  8.7 209.0 %all-gather.9.cloned.1.call-start = ((), (), s32[]{:S(2)}) async-start(), calls=%async_computation.1 | async-start | bytes 3041280 | tf_op jit(solution)/shard_map/all_gather | solution.py:167
  9.4 260.5 %all-gather.11.cloned.1.call-start = ((), (), s32[]{:S(2)}) async-start(), calls=%async_computation.2 | async-start | bytes 5068800 | tf_op jit(solution)/shard_map/all_gather | solution.py:168
  10.7 216.2 %copy-start.3 = (bf16[1,320,2,128]{3,1,2,0:T(8,128)(2,1)}, bf16[1,320,2,128]{3,1,2,0:T(8,128)(2,1)S(1)}, u32[]{:S(2)}) copy-start(bf16[1,320,2,128]{3,1,2,0:T(8,128)(2,1)S(1)} %get-tuple-element.159) | copy-start | bytes 491524
  33.0 118.2 %collective-permute-start = (bf16[1,320,1,128]{3,1,2,0:T(8,128)(2,1)}, bf16[1,320,1,128]{3,1,2,0:T(8,128)(2,1)S(1)}, u32[]{:S(2)}, u32[]{:S(2)}) collective-permute-start(bf16[1,320,1,128]{3,1,2,0:T(8,128)(2,1)} %get-tuple-element.153), channel_id=1, source_target_pairs={{0,1},{1,2},{2,3},{3,4},{4,5},{5,6},{6,7},{8,9},{9,10},{10,11},{11... | collective-permute-start | bytes 245768 | tf_op jit(solution)/shard_map/ppermute | solution.py:20
  34.3 117.5 %collective-permute-start.1 = (bf16[1,320,1,128]{3,1,2,0:T(8,128)(2,1)}, bf16[1,320,1,128]{3,1,2,0:T(8,128)(2,1)}, u32[]{:S(2)}, u32[]{:S(2)}) collective-permute-start(bf16[1,320,1,128]{3,1,2,0:T(8,128)(2,1)} %get-tuple-element.154), channel_id=1, source_target_pairs={{1,0},{2,1},{3,2},{4,3},{5,4},{6,5},{7,6},{9,8},{10,9},{11,10},{12... | collective-permute-start | bytes 245768 | tf_op jit(solution)/shard_map/ppermute | solution.py:21
  37.0 58.6 %copy-start.13 = (bf16[1,320,2,128]{3,1,2,0:T(8,128)(2,1)}, bf16[1,320,2,128]{3,1,2,0:T(8,128)(2,1)S(1)}, u32[]{:S(2)}) copy-start(bf16[1,320,2,128]{3,1,2,0:T(8,128)(2,1)S(1)} %fusion.104) | copy-start | bytes 491524
  37.8 57.9 %copy-start.30 = (bf16[1,320,2,128]{3,2,1,0:T(2,128)(2,1)S(1)}, bf16[1,320,2,128]{3,2,1,0:T(2,128)(2,1)}, u32[]{:S(2)}) copy-start(bf16[1,320,2,128]{3,2,1,0:T(2,128)(2,1)} %param.31) | copy-start | bytes 491524
  37.8 117.3 %collective-permute-start.2 = (bf16[1,320,1,128]{3,1,2,0:T(8,128)(2,1)}, bf16[1,320,1,128]{3,1,2,0:T(8,128)(2,1)}, u32[]{:S(2)}, u32[]{:S(2)}) collective-permute-start(bf16[1,320,1,128]{3,1,2,0:T(8,128)(2,1)} %get-tuple-element.155), channel_id=1, source_target_pairs={{0,1},{1,2},{2,3},{3,4},{4,5},{5,6},{6,7},{8,9},{9,10},{10,11},{11... | collective-permute-start | bytes 245768 | tf_op jit(solution)/shard_map/ppermute | solution.py:20
  43.1 112.0 %collective-permute-start.3 = (bf16[1,320,1,128]{3,1,2,0:T(8,128)(2,1)}, bf16[1,320,1,128]{3,1,2,0:T(8,128)(2,1)}, u32[]{:S(2)}, u32[]{:S(2)}) collective-permute-start(bf16[1,320,1,128]{3,1,2,0:T(8,128)(2,1)} %get-tuple-element.156), channel_id=1, source_target_pairs={{1,0},{2,1},{3,2},{4,3},{5,4},{6,5},{7,6},{9,8},{10,9},{11,10},{12... | collective-permute-start | bytes 245768 | tf_op jit(solution)/shard_map/ppermute | solution.py:21
  44.4 725.3 %all-reduce.17.cloned.1.call-start = ((), (), s32[]{:S(2)}) async-start(), calls=%async_computation.4 | async-start | bytes 24576000
  90.6 8.6 copy-start.31
  98.5 0.7 copy-start.28
  149.6 6.1 copy-start.14
  151.2 0.6 copy-start.22
  155.0 0.7 copy-start.18
  158.9 3.2 copy-start.37
  162.1 2.0 copy-start.20
  186.6 1.4 copy-start.32
  188.9 5.4 copy-start.21
  190.1 24.9 %collective-permute-start.6 = (bf16[1,320,1,128]{3,1,2,0:T(8,128)(2,1)}, bf16[1,320,1,128]{3,1,2,0:T(8,128)(2,1)S(1)}, u32[]{:S(2)}, u32[]{:S(2)}) collective-permute-start(bf16[1,320,1,128]{3,1,2,0:T(8,128)(2,1)} %bitcast.32), channel_id=1, source_target_pairs={{0,1},{1,2},{2,3},{3,4},{4,5},{5,6},{6,7},{8,9},{9,10},{10,11},{11... | collective-permute-start | bytes 245768 | tf_op jit(solution)/shard_map/ppermute | solution.py:20
  191.5 12.2 %copy-start.29 = (bf16[320,2,1,8,17]{0,3,4,1,2:T(8,128)(2,1)S(1)}, bf16[320,2,1,8,17]{0,3,4,1,2:T(8,128)(2,1)}, u32[]{:S(2)}) copy-start(bf16[320,2,1,8,17]{0,3,4,1,2:T(8,128)(2,1)} %copy-done.28) | copy-start | bytes 522244
  191.5 12.2 %copy-start.38 = (pred[8,17]{0,1:T(8,128)(4,1)S(1)}, pred[8,17]{0,1:T(8,128)(4,1)}, u32[]{:S(2)}) copy-start(pred[8,17]{0,1:T(8,128)(4,1)} %constant.237) | copy-start | bytes 412
  192.3 24.1 %collective-permute-start.7 = (bf16[1,320,1,128]{3,1,2,0:T(8,128)(2,1)}, bf16[1,320,1,128]{3,1,2,0:T(8,128)(2,1)S(1)}, u32[]{:S(2)}, u32[]{:S(2)}) collective-permute-start(bf16[1,320,1,128]{3,1,2,0:T(8,128)(2,1)} %bitcast.35), channel_id=1, source_target_pairs={{1,0},{2,1},{3,2},{4,3},{5,4},{6,5},{7,6},{9,8},{10,9},{11,10},{12... | collective-permute-start | bytes 245768 | tf_op jit(solution)/shard_map/ppermute | solution.py:21
  195.6 27.0 %collective-permute-start.5 = (bf16[1,320,1,128]{1,2,3,0:T(2,128)(2,1)}, bf16[1,320,1,128]{1,2,3,0:T(2,128)(2,1)}, u32[]{:S(2)}, u32[]{:S(2)}) collective-permute-start(bf16[1,320,1,128]{1,2,3,0:T(2,128)(2,1)} %slice_bitcast_fusion.16), channel_id=1, source_target_pairs={{1,0},{2,1},{3,2},{4,3},{5,4},{6,5},{7,6},{9,8},{10,9},{11,10},{12... | collective-permute-start | bytes 245768 | tf_op jit(solution)/shard_map/ppermute | solution.py:21
  197.6 23.8 %collective-permute-start.4 = (bf16[1,320,1,128]{1,3,0,2:T(8,128)(2,1)}, bf16[1,320,1,128]{1,3,0,2:T(8,128)(2,1)}, u32[]{:S(2)}, u32[]{:S(2)}) collective-permute-start(bf16[1,320,1,128]{1,3,0,2:T(8,128)(2,1)} %slice_bitcast_fusion.18), channel_id=1, source_target_pairs={{0,1},{1,2},{2,3},{3,4},{4,5},{5,6},{6,7},{8,9},{9,10},{10,11},{11... | collective-permute-start | bytes 245768 | tf_op jit(solution)/shard_map/ppermute | solution.py:20
  208.4 47.6 %collective-permute-start.10 = (f32[1,320,1,128]{1,2,3,0:T(1,128)}, f32[1,320,1,128]{1,2,3,0:T(1,128)}, u32[]{:S(2)}, u32[]{:S(2)}) collective-permute-start(f32[1,320,1,128]{1,2,3,0:T(1,128)} %slice_bitcast_fusion.14), channel_id=1, source_target_pairs={{0,1},{1,2},{2,3},{3,4},{4,5},{5,6},{6,7},{8,9},{9,10},{10,11},{11... | collective-permute-start | bytes 491528 | tf_op jit(solution)/shard_map/ppermute | solution.py:29
  215.0 5.8 copy-start.24
  215.0 46.9 %collective-permute-start.11 = (f32[1,320,1,128]{1,2,3,0:T(1,128)}, f32[1,320,1,128]{1,2,3,0:T(1,128)}, u32[]{:S(2)}, u32[]{:S(2)}) collective-permute-start(f32[1,320,1,128]{1,2,3,0:T(1,128)} %slice_bitcast_fusion.13), channel_id=1, source_target_pairs={{1,0},{2,1},{3,2},{4,3},{5,4},{6,5},{7,6},{9,8},{10,9},{11,10},{12... | collective-permute-start | bytes 491528 | tf_op jit(solution)/shard_map/ppermute | solution.py:29
  216.3 4.5 copy-start.26
  216.9 0.8 copy-start.19
  221.4 3.1 copy-start.35
  225.7 1.3 copy-start.16
  225.7 2.6 copy-start.12
  228.3 27.7 %copy-start.17 = (f32[1,8,17,320]{3,0,2,1:T(1,128)S(1)}, f32[1,8,17,320]{3,0,2,1:T(1,128)}, u32[]{:S(2)}) copy-start(f32[1,8,17,320]{3,0,2,1:T(1,128)} %copy.242) | copy-start | bytes 522244
  253.3 12.7 %collective-permute-start.8 = (bf16[1,640,1,128]{3,1,2,0:T(8,128)(2,1)}, bf16[1,640,1,128]{3,1,2,0:T(8,128)(2,1)S(1)}, u32[]{:S(2)}, u32[]{:S(2)}) collective-permute-start(bf16[1,640,1,128]{3,1,2,0:T(8,128)(2,1)} %get-tuple-element.145), channel_id=1, source_target_pairs={{0,1},{1,2},{2,3},{3,4},{4,5},{5,6},{6,7},{8,9},{9,10},{10,11},{11... | collective-permute-start | bytes 491528 | tf_op jit(solution)/shard_map/ppermute | solution.py:20
  254.6 11.4 %collective-permute-start.9 = (bf16[1,640,1,128]{3,1,2,0:T(8,128)(2,1)}, bf16[1,640,1,128]{3,1,2,0:T(8,128)(2,1)}, u32[]{:S(2)}, u32[]{:S(2)}) collective-permute-start(bf16[1,640,1,128]{3,1,2,0:T(8,128)(2,1)} %get-tuple-element.146), channel_id=1, source_target_pairs={{1,0},{2,1},{3,2},{4,3},{5,4},{6,5},{7,6},{9,8},{10,9},{11,10},{12... | collective-permute-start | bytes 491528 | tf_op jit(solution)/shard_map/ppermute | solution.py:21
  272.8 2.7 copy-start.2
  326.0 7.6 collective-permute-start.12
  328.8 10.8 %copy-start.15 = (f32[1,640,2,128]{3,1,2,0:T(8,128)S(1)}, f32[1,640,2,128]{3,1,2,0:T(8,128)}, u32[]{:S(2)}) copy-start(f32[1,640,2,128]{3,1,2,0:T(8,128)} %get-tuple-element.140) | copy-start | bytes 1966084
  332.3 7.2 collective-permute-start.13
  369.2 3.0 copy-start.39
  375.9 3.4 copy-start.25
  375.9 3.7 copy-start.9
  375.9 3.7 copy-start.10
  376.3 13.4 %collective-permute-start.14 = (f32[1,320,1,128]{1,2,3,0:T(1,128)S(1)}, f32[1,320,1,128]{1,2,3,0:T(1,128)S(1)}, u32[]{:S(2)}, u32[]{:S(2)}) collective-permute-start(f32[1,320,1,128]{1,2,3,0:T(1,128)S(1)} %slice_bitcast_fusion.11), channel_id=1, source_target_pairs={{0,1},{1,2},{2,3},{3,4},{4,5},{5,6},{6,7},{8,9},{9,10},{10,11},{11... | collective-permute-start | bytes 491528 | tf_op jit(solution)/shard_map/ppermute | solution.py:29
  378.5 1.2 copy-start.6
  378.5 1.2 copy-start.7
  378.5 1.4 copy-start.8
  379.6 1.0 copy-start.27
  379.9 1.0 copy-start.5
  381.4 7.3 copy-start.4
  386.9 11.4 %copy-start.11 = (f32[2,8,17,320]{3,0,2,1:T(2,128)S(1)}, f32[2,8,17,320]{3,0,2,1:T(2,128)}, u32[]{:S(2)}) copy-start(f32[2,8,17,320]{3,0,2,1:T(2,128)} %copy.271) | copy-start | bytes 1044484
  387.1 8.1 collective-permute-start.15
  389.9 32.0 %copy-start.33 = (f32[320]{0:T(512)S(1)}, f32[320]{0:T(512)}, u32[]{:S(2)}) copy-start(f32[320]{0:T(512)} %copy-done.32) | copy-start | bytes 3844
  423.2 1.7 copy-start.23
  432.4 0.7 copy-start.36
  432.5 429.8 %copy-start.1 = (bf16[320,3,3,320]{3,0,2,1:T(8,128)(2,1)S(1)}, bf16[320,3,3,320]{3,0,2,1:T(8,128)(2,1)}, u32[]{:S(2)}) copy-start(bf16[320,3,3,320]{3,0,2,1:T(8,128)(2,1)} %param.38) | copy-start | bytes 5529604
  432.5 426.5 %all-reduce.19.cloned.1.call-start = ((), (), s32[]{:S(2)}) async-start(), calls=%async_computation.5 | async-start | bytes 737280 | tf_op jit(solution)/shard_map/psum | solution.py:225
Sparse Core Ops, SparseCore 0:
  10.6 58.0 all-gather.6
  71.3 54.9 all-gather.12
  129.0 55.0 all-gather.8
  186.5 60.2 all-gather.10
  432.6 337.0 all-reduce.16
  773.1 85.8 all-reduce.18
where the time goes:
time: 879 us; the launch traced here: 869 us
  waiting for transfers between devices  393 us (45%)
  blocking collectives  277 us (32%)
  local copies, waits for them, and re-layouts  76.4 us (9%)
  matrix products  46.1 us (5%)
  starting transfers between devices  33.6 us (4%)
  other arithmetic  25.6 us (3%)
  between operations  17.4 us (2%)
    unnamed x7, waiting for transfers between devices  337 us
    psum x4, blocking collectives, group_norm(): lax.psum((jnp.sum(grouped, axis=(2, 3, 4)), jnp.sum(grouped * grouped, ax...  85.1 us
    psum x3, blocking collectives, norm_back(): lax.psum((jnp.sum(grouped, axis=(2, 3, 4)), jnp.sum(grouped * normed_grou...  61.5 us
    all_gather x1, blocking collectives, per_device(): lax.all_gather(dec_shortcut, 'dp', axis=0, tiled=True)  49.5 us
    psum x1, waiting for transfers between devices, per_device(): lax.psum((owned[0], owned[1], owned[2]), 'rows')  48.1 us
    all_gather x1, blocking collectives, per_device(): lax.all_gather(zero_conv, 'dp', axis=0, tiled=True)  43.7 us
    psum x1, blocking collectives, per_device(): lax.psum((owned[0], owned[1], owned[2]), 'rows')  37.2 us
    unnamed x105, local copies, waits for them, and re-layouts  24.9 us
  transfers between devices with their start and end apart: 22, of which 4 were waited for; matrix products, arithmetic and copies ran while one was open for 10% of the time, Pallas kernels for 0%

commit v1 on v0

--- a/solution.py
+++ b/solution.py
@@ -1,3 +1,4 @@
+import functools
 import math
 import jax
 import jax.numpy as jnp
@@ -8,6 +9,21 @@
 GROUPS = 32
 EPSILON = 1e-05
 LAYOUT = ("NCHW", "OHWI", "NCHW")
+
+
+def unite_the_tails(arr_in, bus_axis):
+    return jnp.concatenate(
+        lax.all_to_all(
+            jnp.stack([arr_in for _ in range(lax.psum(1, bus_axis))], 0),
+            bus_axis,
+            split_axis=0,
+            concat_axis=0,
+        ),
+        0,
+    )
+
+
+lead_forms_on_mesh = functools.partial(unite_the_tails, bus_axis="dp")
 
 
 def extended(x, sides, width):
@@ -167,7 +183,7 @@
         lax.all_gather(ctl_conv_two, "dp", axis=0, tiled=True),
         lax.all_gather(dec_conv_one, "dp", axis=0, tiled=True),
         lax.all_gather(dec_conv_two, "dp", axis=0, tiled=True),
-        lax.all_gather(dec_shortcut, "dp", axis=0, tiled=True),
+        lead_forms_on_mesh(dec_shortcut),
         lax.all_gather(zero_conv, "dp", axis=0, tiled=True),
     )
     half_width = C // 2

time: 879 us -> 872 us (level)
  blocking collectives: 277 us -> 233 us
  local copies, waits for them, and re-layouts: 76.4 us -> 95.8 us
  starting transfers between devices: 33.6 us -> 48.8 us
    all_gather x1 -> x0, blocking collectives: 49.5 us -> none  [per_device(): lax.all_gather(dec_shortcut, 'dp', axis=0, tiled=True)]
    all_to_all x0 -> x1, starting transfers between devices: none -> 10.8 us  [unite_the_tails(): lax.all_to_all(jnp.stack([arr_in for _ in range(lax.psum(1, bus_axis))],...]
    unnamed x105 -> x112, local copies, waits for them, and re-layouts: 24.9 us -> 33.3 us
  transfers between devices with their start and end apart: 22 -> 23, of which waited for: 4 -> 5; matrix products, arithmetic and copies ran while one was open for 10% -> 12% of each run, Pallas kernels for 0% -> 0%
where the time goes in v1:
time: 872 us; the launch traced here: 862 us
  waiting for transfers between devices  398 us (46%)
  blocking collectives  233 us (27%)
  local copies, waits for them, and re-layouts  95.8 us (11%)
  starting transfers between devices  48.8 us (6%)
  matrix products  45 us (5%)
  other arithmetic  24 us (3%)
  between operations  17.3 us (2%)
    unnamed x7, waiting for transfers between devices  339 us
    psum x4, blocking collectives, group_norm(): lax.psum((jnp.sum(grouped, axis=(2, 3, 4)), jnp.sum(grouped * grouped, ax...  83.7 us
    psum x3, blocking collectives, norm_back(): lax.psum((jnp.sum(grouped, axis=(2, 3, 4)), jnp.sum(grouped * normed_grou...  60 us
    all_gather x1, blocking collectives, per_device(): lax.all_gather(zero_conv, 'dp', axis=0, tiled=True)  52 us
    psum x1, waiting for transfers between devices, per_device(): lax.psum((owned[0], owned[1], owned[2]), 'rows')  48.1 us
    psum x1, blocking collectives, per_device(): lax.psum((owned[0], owned[1], owned[2]), 'rows')  37.2 us
    unnamed x112, local copies, waits for them, and re-layouts  33.3 us
    conv_general_dilated x8, matrix products, conv_rows(): lax.conv_general_dilated(padded, weight, (1, 1), ((0, 0), (1, 1)), dimens...  22.8 us
  transfers between devices with their start and end apart: 23, of which 5 were waited for; matrix products, arithmetic and copies ran while one was open for 12% of the time, Pallas kernels for 0%

profile of v1, /device:TPU:8, one launch (start us, length us, event | category | flops | bytes accessed | tf_op | source)
XLA Modules:
  0.0 861.9 jit_solution(1293333744009754316)
XLA Ops:
  11.6 20.1 %all-reduce.12 = (f32[1,32]{1,0:T(1,128)S(1)}, f32[1,32]{1,0:T(1,128)S(1)}, f32[1,32]{1,0:T(1,128)S(1)}, f32[1,32]{1,0:T(1,128)S(1)}) all-reduce(f32[1,32]{1,0:T(1,128)S(1)} %bitcast.481, f32[1,32]{1,0:T(1,128)S(1)} %bitcast.476, f32[1,32]{1,0:T(1,128)S(1)} %bitcast.479, ...), channel_id=1, replica_groups=mesh['dp'=32,'rows'=8] {'rows'}, use_global_device_ids=true, to_apply=%region_5.6 | all-reduce | flops 128 | bytes 1024 | tf_op jit(solution)/shard_map/psum | solution.py:81
  33.0 1.9 collective-permute-start
  39.0 5.2 collective-permute-start.2
  46.4 10.8 %all-to-all-start = ((bf16[32,10,640]{2,1,0:T(8,128)(2,1)}), bf16[32,10,640]{2,1,0:T(8,128)(2,1)S(1)}, u32[]{:S(2)}, u32[]{:S(2)}) async-start(bf16[32,10,640]{2,1,0:T(8,128)(2,1)} %stack.131), calls=%async_computation | async-start | bytes 1310720 | tf_op jit(solution)/shard_map/all_to_all | solution.py:16
  58.6 1.4 convolution_reduce_fusion
  60.9 52.0 %all-gather = bf16[32,10,320]{2,1,0:T(8,128)(2,1)S(1)} all-gather(bf16[1,10,320]{2,1,0:T(8,128)(2,1)S(1)} %bitcast.473), channel_id=1, replica_groups=mesh['dp'=32,'rows'=8] {'dp'}, dimensions={0}, use_global_device_ids=true | all-gather | bytes 211200 | tf_op jit(solution)/shard_map/all_gather | solution.py:187
  114.6 1.6 copy.232
  118.9 1.5 convolution_reduce_fusion.3
  120.4 1.5 convolution_reduce_fusion.2
  122.2 1.7 pad_maximum_fusion.2
  123.9 1.9 copy.296
  128.4 1.8 maximum_bitcast_fusion.8
  130.2 2.0 copy.297
  135.7 3.2 fusion.27
  139.0 2.6 select_reduce_fusion.3
  143.8 20.5 %all-reduce.11 = (f32[1,32]{1,0:T(1,128)S(1)}, f32[1,32]{1,0:T(1,128)S(1)}, f32[1,32]{1,0:T(1,128)S(1)}, f32[1,32]{1,0:T(1,128)S(1)}) all-reduce(f32[1,32]{1,0:T(1,128)S(1)} %bitcast.480, f32[1,32]{1,0:T(1,128)S(1)} %bitcast.482, f32[1,32]{1,0:T(1,128)S(1)} %bitcast.478, ...), channel_id=1, replica_groups=mesh['dp'=32,'rows'=8] {'rows'}, use_global_device_ids=true, to_apply=%region_8.9 | all-reduce | flops 128 | bytes 1024 | tf_op jit(solution)/shard_map/psum | solution.py:81
  166.4 1.3 collective-permute-start.6
  168.0 1.3 collective-permute-start.7
  173.4 6.0 collective-permute-start.4
  179.4 3.7 fusion.14
  184.2 4.0 collective-permute-start.10
  191.5 1.3 collective-permute-start.11
  194.0 3.0 fusion.20
  198.7 1.7 maximum_bitcast_fusion.7
  203.0 1.9 copy.286
  204.9 1.4 fusion.34
  207.0 21.8 %all-reduce.10 = (f32[1,32]{1,0:T(1,128)S(1)}, f32[1,32]{1,0:T(1,128)S(1)}) all-reduce(f32[1,32]{1,0:T(1,128)S(1)} %bitcast.484, f32[1,32]{1,0:T(1,128)S(1)} %bitcast.489), channel_id=1, replica_groups=mesh['dp'=32,'rows'=8] {'rows'}, use_global_device_ids=true, to_apply=%region_26.27 | all-reduce | flops 64 | bytes 512 | tf_op jit(solution)/shard_map/psum | solution.py:81
  229.2 2.1 multiply_convert_fusion
  232.0 4.6 collective-permute-start.8
  236.6 1.5 collective-permute-start.9
  238.1 1.8 fusion.131
  239.9 4.0 scatter-add.20
  245.1 2.8 scatter-add.21
  248.0 2.0 maximum_bitcast_fusion.6
  250.0 2.1 copy.299
  252.1 1.4 pad.33.clone
  254.5 2.9 all-gather.10.cloned.1.call-done
  257.4 3.0 copy.236
  260.5 1.9 select_reduce_fusion.1
  262.8 21.3 %all-reduce.9 = (f32[1,32]{1,0:T(1,128)S(1)}, f32[1,32]{1,0:T(1,128)S(1)}) all-reduce(f32[1,32]{1,0:T(1,128)S(1)} %bitcast.486, f32[1,32]{1,0:T(1,128)S(1)} %bitcast.490), channel_id=1, replica_groups=mesh['dp'=32,'rows'=8] {'rows'}, use_global_device_ids=true, to_apply=%region_32.33 | all-reduce | flops 64 | bytes 512 | tf_op jit(solution)/shard_map/psum | solution.py:81
  286.0 18.0 %all-reduce.8 = (f32[1,32]{1,0:T(1,128)S(1)}, f32[1,32]{1,0:T(1,128)S(1)}) all-reduce(f32[1,32]{1,0:T(1,128)S(1)} %bitcast.491, f32[1,32]{1,0:T(1,128)S(1)} %bitcast.485), channel_id=1, replica_groups=mesh['dp'=32,'rows'=8] {'rows'}, use_global_device_ids=true, to_apply=%region_41.42 | all-reduce | flops 64 | bytes 512 | tf_op jit(solution)/shard_map/psum | solution.py:100
  305.1 3.5 fusion.17
  311.5 2.6 collective-permute-start.12
  316.9 1.7 copy.292
  320.5 1.7 copy.294
  324.5 5.1 collective-permute-done.13
  331.0 19.9 %all-reduce.7 = (f32[1,16]{1,0:T(1,128)S(1)}, f32[1,16]{1,0:T(1,128)S(1)}) all-reduce(f32[1,16]{1,0:T(1,128)S(1)} %bitcast.492, f32[1,16]{1,0:T(1,128)S(1)} %bitcast.487), channel_id=1, replica_groups=mesh['dp'=32,'rows'=8] {'rows'}, use_global_device_ids=true, to_apply=%region_47.48 | all-reduce | flops 32 | bytes 256 | tf_op jit(solution)/shard_map/psum | solution.py:100
  351.3 1.7 fusion.35
  362.6 3.7 fusion.11
  366.7 1.7 collective-permute-start.14
  371.9 5.5 copy.283
  377.7 1.5 collective-permute-start.15
  380.5 2.8 scatter-add.26
  383.3 2.5 collective-permute-done.15
  386.1 2.8 scatter-add.29
  389.7 22.2 %all-reduce.6 = (f32[1,32]{1,0:T(1,128)S(1)}, f32[1,32]{1,0:T(1,128)S(1)}) all-reduce(f32[1,32]{1,0:T(1,128)S(1)} %bitcast.488, f32[1,32]{1,0:T(1,128)S(1)} %bitcast.483), channel_id=1, replica_groups=mesh['dp'=32,'rows'=8] {'rows'}, use_global_device_ids=true, to_apply=%region_53.54 | all-reduce | flops 64 | bytes 512 | tf_op jit(solution)/shard_map/psum | solution.py:100
  418.1 5.5 copy.282
  425.6 336.7 %all-reduce.17.cloned.1.call-done = (f32[320,3,3,320]{3,2,1,0:T(4,128)}, f32[320,3,3,320]{3,2,1,0:T(4,128)}, f32[320,320]{1,0:T(8,128)}) async-done(((f32[320,3,3,320]{3,2,1,0:T(4,128)}, f32[320,3,3,320]{3,2,1,0:T(4,128)}, f32[320,320]{1,0:T(8,128)}), (f32[320,3,3,320]{3,2,1,0:T(4,128)}, f32[320,3,3,320]{3,2,1,0:T(4,128)}, f32[320,320]{1,0:T(8,128)})) %all-reduce.17.cloned.1.call-update) | async-done | bytes 7782416
  762.3 1.6 constant_dynamic-slice_fusion.1
  763.9 1.6 constant_dynamic-slice_fusion.2
  766.3 37.2 %psum.167 = f32[10,320]{1,0:T(8,128)} all-reduce(f32[10,320]{1,0:T(8,128)S(1)} %constant_dynamic-slice_fusion), channel_id=1, replica_groups=mesh['dp'=32,'rows'=8] {'rows'}, use_global_device_ids=true, to_apply=%region_59.60 | all-reduce | flops 3200 | bytes 25600 | tf_op jit(solution)/shard_map/psum | solution.py:241
  803.5 48.1 %all-reduce.19.cloned.1.call-done = (f32[10,3,3,320]{3,2,1,0:T(4,128)}, f32[10,3,3,320]{3,2,1,0:T(4,128)}) async-done(((f32[10,3,3,320]{3,2,1,0:T(4,128)}, f32[10,3,3,320]{3,2,1,0:T(4,128)}), (f32[10,3,3,320]{3,2,1,0:T(4,128)}, f32[10,3,3,320]{3,2,1,0:T(4,128)})) %all-reduce.19.cloned.1.call-update) | async-done | bytes 230416 | tf_op jit(solution)/shard_map/psum | solution.py:241
  851.6 1.6 copy.342
  853.2 1.6 copy.343
  (365 shorter events, 85.4 us)
Async XLA Ops:
  7.2 131.8 %copy-start = (bf16[320,3,3,320]{3,0,2,1:T(8,128)(2,1)S(1)}, bf16[320,3,3,320]{3,0,2,1:T(8,128)(2,1)}, u32[]{:S(2)}) copy-start(bf16[320,3,3,320]{3,0,2,1:T(8,128)(2,1)} %param.38) | copy-start | bytes 5529604
  7.2 38.3 %copy-start.37 = (bf16[10,640]{1,0:T(8,128)(2,1)S(1)}, bf16[10,640]{1,0:T(8,128)(2,1)}, u32[]{:S(2)}) copy-start(bf16[10,640]{1,0:T(8,128)(2,1)} %param.44) | copy-start | bytes 38404
  7.2 128.5 %all-gather.6.cloned.1.call-start = ((), (), s32[]{:S(2)}) async-start(), calls=%async_computation.1 | async-start | bytes 3041280 | tf_op jit(solution)/shard_map/all_gather | solution.py:182
  7.9 171.4 %all-gather.12.cloned.1.call-start = ((), (), s32[]{:S(2)}) async-start(), calls=%async_computation.4 | async-start | bytes 3041280 | tf_op jit(solution)/shard_map/all_gather | solution.py:185
  8.7 185.3 %all-gather.8.cloned.1.call-start = ((), (), s32[]{:S(2)}) async-start(), calls=%async_computation.2 | async-start | bytes 3041280 | tf_op jit(solution)/shard_map/all_gather | solution.py:183
  10.7 49.3 %copy-start.3 = (bf16[1,320,2,128]{3,1,2,0:T(8,128)(2,1)}, bf16[1,320,2,128]{3,1,2,0:T(8,128)(2,1)S(1)}, u32[]{:S(2)}) copy-start(bf16[1,320,2,128]{3,1,2,0:T(8,128)(2,1)S(1)} %get-tuple-element.159) | copy-start | bytes 491524
  32.0 28.0 %copy-start.34 = (bf16[1,320,2,128]{3,2,1,0:T(2,128)(2,1)S(1)}, bf16[1,320,2,128]{3,2,1,0:T(2,128)(2,1)}, u32[]{:S(2)}) copy-start(bf16[1,320,2,128]{3,2,1,0:T(2,128)(2,1)} %param.32) | copy-start | bytes 491524
  32.3 28.7 %copy-start.38 = (bf16[10,320]{1,0:T(8,128)(2,1)S(1)}, bf16[10,320]{1,0:T(8,128)(2,1)}, u32[]{:S(2)}) copy-start(bf16[10,320]{1,0:T(8,128)(2,1)} %param.45) | copy-start | bytes 19204
  33.0 89.2 %collective-permute-start = (bf16[1,320,1,128]{3,1,2,0:T(8,128)(2,1)}, bf16[1,320,1,128]{3,1,2,0:T(8,128)(2,1)}, u32[]{:S(2)}, u32[]{:S(2)}) collective-permute-start(bf16[1,320,1,128]{3,1,2,0:T(8,128)(2,1)} %get-tuple-element.153), channel_id=1, source_target_pairs={{0,1},{1,2},{2,3},{3,4},{4,5},{5,6},{6,7},{8,9},{9,10},{10,11},{11... | collective-permute-start | bytes 245768 | tf_op jit(solution)/shard_map/ppermute | solution.py:36
  34.9 87.3 %collective-permute-start.1 = (bf16[1,320,1,128]{3,1,2,0:T(8,128)(2,1)}, bf16[1,320,1,128]{3,1,2,0:T(8,128)(2,1)S(1)}, u32[]{:S(2)}, u32[]{:S(2)}) collective-permute-start(bf16[1,320,1,128]{3,1,2,0:T(8,128)(2,1)} %get-tuple-element.154), channel_id=1, source_target_pairs={{1,0},{2,1},{3,2},{4,3},{5,4},{6,5},{7,6},{9,8},{10,9},{11,10},{12... | collective-permute-start | bytes 245768 | tf_op jit(solution)/shard_map/ppermute | solution.py:37
  39.0 89.4 %collective-permute-start.2 = (bf16[1,320,1,128]{3,1,2,0:T(8,128)(2,1)}, bf16[1,320,1,128]{3,1,2,0:T(8,128)(2,1)}, u32[]{:S(2)}, u32[]{:S(2)}) collective-permute-start(bf16[1,320,1,128]{3,1,2,0:T(8,128)(2,1)} %get-tuple-element.155), channel_id=1, source_target_pairs={{0,1},{1,2},{2,3},{3,4},{4,5},{5,6},{6,7},{8,9},{9,10},{10,11},{11... | collective-permute-start | bytes 245768 | tf_op jit(solution)/shard_map/ppermute | solution.py:36
  44.2 84.3 %collective-permute-start.3 = (bf16[1,320,1,128]{3,1,2,0:T(8,128)(2,1)}, bf16[1,320,1,128]{3,1,2,0:T(8,128)(2,1)}, u32[]{:S(2)}, u32[]{:S(2)}) collective-permute-start(bf16[1,320,1,128]{3,1,2,0:T(8,128)(2,1)} %get-tuple-element.156), channel_id=1, source_target_pairs={{1,0},{2,1},{3,2},{4,3},{5,4},{6,5},{7,6},{9,8},{10,9},{11,10},{12... | collective-permute-start | bytes 245768 | tf_op jit(solution)/shard_map/ppermute | solution.py:37
  46.4 88.5 %all-to-all-start = ((bf16[32,10,640]{2,1,0:T(8,128)(2,1)}), bf16[32,10,640]{2,1,0:T(8,128)(2,1)S(1)}, u32[]{:S(2)}, u32[]{:S(2)}) async-start(bf16[32,10,640]{2,1,0:T(8,128)(2,1)} %stack.131), calls=%async_computation | async-start | bytes 1310720 | tf_op jit(solution)/shard_map/all_to_all | solution.py:16
  57.1 200.3 %all-gather.10.cloned.1.call-start = ((), (), s32[]{:S(2)}) async-start(), calls=%async_computation.3 | async-start | bytes 5068800 | tf_op jit(solution)/shard_map/all_gather | solution.py:184
  57.7 704.5 %all-reduce.17.cloned.1.call-start = ((), (), s32[]{:S(2)}) async-start(), calls=%async_computation.5 | async-start | bytes 24576000
  117.4 4.5 copy-start.20
  122.2 10.0 %copy-start.28 = (bf16[1,320,1,128]{3,1,2,0:T(8,128)(2,1)}, bf16[1,320,1,128]{3,1,2,0:T(8,128)(2,1)S(1)}, u32[]{:S(2)}) copy-start(bf16[1,320,1,128]{3,1,2,0:T(8,128)(2,1)S(1)} %collective-permute-done.1) | copy-start | bytes 245764
  127.1 0.7 copy-start.24
  127.8 7.9 copy-start.41
  133.4 0.8 copy-start.25
  135.7 3.2 copy-start.26
  135.7 3.2 copy-start.35
  135.7 3.2 copy-start.42
  165.8 4.2 copy-start.27
  166.4 25.1 %collective-permute-start.6 = (bf16[1,320,1,128]{3,1,2,0:T(8,128)(2,1)S(1)}, bf16[1,320,1,128]{3,1,2,0:T(8,128)(2,1)S(1)}, u32[]{:S(2)}, u32[]{:S(2)}) collective-permute-start(bf16[1,320,1,128]{3,1,2,0:T(8,128)(2,1)S(1)} %bitcast.471), channel_id=1, source_target_pairs={{0,1},{1,2},{2,3},{3,4},{4,5},{5,6},{6,7},{8,9},{9,10},{10,11},{11... | collective-permute-start | bytes 245768 | tf_op jit(solution)/shard_map/ppermute | solution.py:36
  167.8 11.6 %copy-start.33 = (bf16[320,2,1,8,17]{0,3,4,1,2:T(8,128)(2,1)S(1)}, bf16[320,2,1,8,17]{0,3,4,1,2:T(8,128)(2,1)}, u32[]{:S(2)}) copy-start(bf16[320,2,1,8,17]{0,3,4,1,2:T(8,128)(2,1)} %copy-done.32) | copy-start | bytes 522244
  167.8 11.6 %copy-start.36 = (bf16[320,2,1,7,2]{0,3,4,1,2:T(8,128)(2,1)S(1)}, bf16[320,2,1,7,2]{0,3,4,1,2:T(8,128)(2,1)}, u32[]{:S(2)}) copy-start(bf16[320,2,1,7,2]{0,3,4,1,2:T(8,128)(2,1)} %slice.424) | copy-start | bytes 53764
  167.8 11.6 %copy-start.43 = (pred[8,17]{0,1:T(8,128)(4,1)S(1)}, pred[8,17]{0,1:T(8,128)(4,1)}, u32[]{:S(2)}) copy-start(pred[8,17]{0,1:T(8,128)(4,1)} %constant.237) | copy-start | bytes 412
  168.0 24.8 %collective-permute-start.7 = (bf16[1,320,1,128]{3,1,2,0:T(8,128)(2,1)S(1)}, bf16[1,320,1,128]{3,1,2,0:T(8,128)(2,1)S(1)}, u32[]{:S(2)}, u32[]{:S(2)}) collective-permute-start(bf16[1,320,1,128]{3,1,2,0:T(8,128)(2,1)S(1)} %bitcast.472), channel_id=1, source_target_pairs={{1,0},{2,1},{3,2},{4,3},{5,4},{6,5},{7,6},{9,8},{10,9},{11,10},{12... | collective-permute-start | bytes 245768 | tf_op jit(solution)/shard_map/ppermute | solution.py:37
  171.3 27.4 %collective-permute-start.5 = (bf16[1,320,1,128]{1,2,3,0:T(2,128)(2,1)}, bf16[1,320,1,128]{1,2,3,0:T(2,128)(2,1)}, u32[]{:S(2)}, u32[]{:S(2)}) collective-permute-start(bf16[1,320,1,128]{1,2,3,0:T(2,128)(2,1)} %slice_bitcast_fusion.16), channel_id=1, source_target_pairs={{1,0},{2,1},{3,2},{4,3},{5,4},{6,5},{7,6},{9,8},{10,9},{11,10},{12... | collective-permute-start | bytes 245768 | tf_op jit(solution)/shard_map/ppermute | solution.py:37
  173.4 24.2 %collective-permute-start.4 = (bf16[1,320,1,128]{1,3,0,2:T(8,128)(2,1)}, bf16[1,320,1,128]{1,3,0,2:T(8,128)(2,1)}, u32[]{:S(2)}, u32[]{:S(2)}) collective-permute-start(bf16[1,320,1,128]{1,3,0,2:T(8,128)(2,1)} %slice_bitcast_fusion.18), channel_id=1, source_target_pairs={{0,1},{1,2},{2,3},{3,4},{4,5},{5,6},{6,7},{8,9},{9,10},{10,11},{11... | collective-permute-start | bytes 245768 | tf_op jit(solution)/shard_map/ppermute | solution.py:36
  184.2 53.9 %collective-permute-start.10 = (f32[1,320,1,128]{1,2,3,0:T(1,128)}, f32[1,320,1,128]{1,2,3,0:T(1,128)}, u32[]{:S(2)}, u32[]{:S(2)}) collective-permute-start(f32[1,320,1,128]{1,2,3,0:T(1,128)} %slice_bitcast_fusion.14), channel_id=1, source_target_pairs={{0,1},{1,2},{2,3},{3,4},{4,5},{5,6},{6,7},{8,9},{9,10},{10,11},{11... | collective-permute-start | bytes 491528 | tf_op jit(solution)/shard_map/ppermute | solution.py:45
  191.5 52.4 %collective-permute-start.11 = (f32[1,320,1,128]{1,2,3,0:T(1,128)}, f32[1,320,1,128]{1,2,3,0:T(1,128)}, u32[]{:S(2)}, u32[]{:S(2)}) collective-permute-start(f32[1,320,1,128]{1,2,3,0:T(1,128)} %slice_bitcast_fusion.13), channel_id=1, source_target_pairs={{1,0},{2,1},{3,2},{4,3},{5,4},{6,5},{7,6},{9,8},{10,9},{11,10},{12... | collective-permute-start | bytes 491528 | tf_op jit(solution)/shard_map/ppermute | solution.py:45
  197.5 3.2 copy-start.39
  201.9 3.0 copy-start.4
  201.9 4.4 copy-start.15
  203.0 35.1 %copy-start.21 = (f32[1,8,17,320]{3,0,2,1:T(1,128)S(1)}, f32[1,8,17,320]{3,0,2,1:T(1,128)}, u32[]{:S(2)}) copy-start(f32[1,8,17,320]{3,0,2,1:T(1,128)} %copy.242) | copy-start | bytes 522244
  232.0 16.0 %collective-permute-start.8 = (bf16[1,640,1,128]{3,1,2,0:T(8,128)(2,1)}, bf16[1,640,1,128]{3,1,2,0:T(8,128)(2,1)}, u32[]{:S(2)}, u32[]{:S(2)}) collective-permute-start(bf16[1,640,1,128]{3,1,2,0:T(8,128)(2,1)} %get-tuple-element.145), channel_id=1, source_target_pairs={{0,1},{1,2},{2,3},{3,4},{4,5},{5,6},{6,7},{8,9},{9,10},{10,11},{11... | collective-permute-start | bytes 491528 | tf_op jit(solution)/shard_map/ppermute | solution.py:36
  236.6 11.4 %collective-permute-start.9 = (bf16[1,640,1,128]{3,1,2,0:T(8,128)(2,1)}, bf16[1,640,1,128]{3,1,2,0:T(8,128)(2,1)}, u32[]{:S(2)}, u32[]{:S(2)}) collective-permute-start(bf16[1,640,1,128]{3,1,2,0:T(8,128)(2,1)} %get-tuple-element.146), channel_id=1, source_target_pairs={{1,0},{2,1},{3,2},{4,3},{5,4},{6,5},{7,6},{9,8},{10,9},{11,10},{12... | collective-permute-start | bytes 491528 | tf_op jit(solution)/shard_map/ppermute | solution.py:37
  253.6 0.9 copy-start.18
  257.4 3.0 copy-start.19
  260.5 1.9 copy-start.2
  308.7 0.9 copy-start.13
  310.4 4.0 slice-start
  311.5 12.0 %collective-permute-start.12 = (f32[1,320,1,128]{3,1,2,0:T(8,128)}, f32[1,320,1,128]{3,1,2,0:T(8,128)}, u32[]{:S(2)}, u32[]{:S(2)}) collective-permute-start(f32[1,320,1,128]{3,1,2,0:T(8,128)} %bitcast.86), channel_id=1, source_target_pairs={{0,1},{1,2},{2,3},{3,4},{4,5},{5,6},{6,7},{8,9},{9,10},{10,11},{11... | collective-permute-start | bytes 491528 | tf_op jit(solution)/shard_map/ppermute | solution.py:45
  314.9 14.8 %copy-start.17 = (f32[1,640,2,128]{3,1,2,0:T(8,128)S(1)}, f32[1,640,2,128]{3,1,2,0:T(8,128)}, u32[]{:S(2)}) copy-start(f32[1,640,2,128]{3,1,2,0:T(8,128)} %get-tuple-element.140) | copy-start | bytes 1966084
  322.2 7.5 collective-permute-start.13
  352.9 5.9 copy-start.22
  366.3 3.6 copy-start.11
  366.3 3.6 copy-start.12
  366.7 13.6 %collective-permute-start.14 = (f32[1,320,1,128]{1,2,3,0:T(1,128)S(1)}, f32[1,320,1,128]{1,2,3,0:T(1,128)S(1)}, u32[]{:S(2)}, u32[]{:S(2)}) collective-permute-start(f32[1,320,1,128]{1,2,3,0:T(1,128)S(1)} %slice_bitcast_fusion.11), channel_id=1, source_target_pairs={{0,1},{1,2},{2,3},{3,4},{4,5},{5,6},{6,7},{8,9},{9,10},{10,11},{11... | collective-permute-start | bytes 491528 | tf_op jit(solution)/shard_map/ppermute | solution.py:45
  368.9 1.2 copy-start.8
  368.9 1.2 copy-start.9
  368.9 1.4 copy-start.10
  370.0 1.0 copy-start.31
  370.3 1.0 copy-start.6
  370.3 1.2 copy-start.7
  371.9 7.3 copy-start.5
  371.9 7.3 copy-start.23
  377.5 11.4 %copy-start.14 = (f32[2,8,17,320]{3,0,2,1:T(2,128)S(1)}, f32[2,8,17,320]{3,0,2,1:T(2,128)}, u32[]{:S(2)}) copy-start(f32[2,8,17,320]{3,0,2,1:T(2,128)} %copy.271) | copy-start | bytes 1044484
  377.7 8.1 collective-permute-start.15
  416.6 0.9 copy-start.29
  423.7 431.1 %copy-start.1 = (bf16[320,3,3,320]{3,0,2,1:T(8,128)(2,1)S(1)}, bf16[320,3,3,320]{3,0,2,1:T(8,128)(2,1)}, u32[]{:S(2)}) copy-start(bf16[320,3,3,320]{3,0,2,1:T(8,128)(2,1)} %param.38) | copy-start | bytes 5529604
  423.7 427.9 %all-reduce.19.cloned.1.call-start = ((), (), s32[]{:S(2)}) async-start(), calls=%async_computation.6 | async-start | bytes 737280 | tf_op jit(solution)/shard_map/psum | solution.py:241
  (4 other events, 2.6 us)
Sparse Core Ops, SparseCore 0:
  10.6 60.4 all-gather.5
  73.7 62.7 all-gather.11
  139.1 53.3 all-gather.7
  194.9 62.4 all-gather.9
  423.8 338.3 all-reduce.16
  765.7 85.8 all-reduce.18
